TPU v7x, 256 devices: a whole 4x4x8 slice. The times are simulated.
256 devices in a mesh: emb: 32 (over z_hi, y, core), wide: 8 (over x, z_lo).
Axes of the slice: x: 4, y: 4, z: 8 (z_hi: 4, z_lo: 2; z = z_hi * 2 + z_lo), core: 2. Of those that a mesh axis runs over, the one named last changes fastest.
Arguments:
- tables: bfloat16 [512, 512, 256], P('emb'), may hold values from -3 to 3
- bag_ids: int32 [8, 128, 512, 4], P('wide', None, 'emb'), may hold values from 0 to 511
- bag_lengths: int32 [8, 128, 512], P('wide', None, 'emb'), may hold values from 1 to 4
- slot_field: int32 [512], replicated, may hold values from 0 to 511, each once
- proj_y: bfloat16 [512, 256], replicated, may hold values from -0.25 to 0.25
- proj_p: bfloat16 [128, 512], replicated, may hold values from -0.25 to 0.25
- linear_w: bfloat16 [384, 512], replicated, may hold values from -0.25 to 0.25
- fm_gain: float32 [256], replicated, may hold values from 0.5 to 1.5
- w_up: bfloat16 [8192, 256], P('wide'), may hold values from -0.375 to 0.375
- w_down: bfloat16 [8192, 256], P('wide'), may hold values from -0.0625 to 0.0625
- out_gain: float32 [256], replicated, may hold values from 0.5 to 1.5
- cotangent: bfloat16 [8, 128, 512, 256], P('wide', 'emb'), may hold values from -6 to 6
Outputs:
- layer_out: bfloat16 [8, 128, 512, 256], P('wide', 'emb')
- pooled_grad: bfloat16 [8, 128, 512, 256], P('wide', None, 'emb')
- grad_up: float32 [8192, 256], P('wide')
- grad_down: float32 [8192, 256], P('wide')
Inputs may be any that keep to these rules, and one draw needn't show every extreme that they name: `bag_ids`: each id indexes a bucket of the table of its slot. `slot_field`: each field appears in exactly one slot.
All inputs are finite; a program needn't handle non-finite values.
Results may differ from a plain program's by a relative error of at most 0.008.
Values may be sent and summed in bfloat16 or wider, within the bound.
A program may use at most 128 MiB of HBM per device.

v0:
```python
import jax
import jax.numpy as jnp
from jax import lax
from jax.sharding import PartitionSpec as P

NF = 128
norm_eps = 1e-05


def layer_norm(values):
    centre = jnp.mean(values, axis=-1, keepdims=True)
    shifted = values - centre
    scale = lax.rsqrt(jnp.mean(shifted * shifted, axis=-1, keepdims=True) + norm_eps)
    return (shifted * scale, scale)


def norm_back(unit, scale, gain, upstream):
    scaled = upstream * gain
    return scale * (
        scaled
        - jnp.mean(scaled, axis=-1, keepdims=True)
        - unit * jnp.mean(scaled * unit, axis=-1, keepdims=True)
    )


def silu_back(values):
    sigma = jax.nn.sigmoid(values)
    return sigma * (1.0 + values * (1.0 - sigma))


def pool_bags(tables, ids, lengths):
    slots_here = tables.shape[0]
    bucket_count = tables.shape[1]
    flat_ids = ids + (jnp.arange(slots_here, dtype=jnp.int32) * bucket_count)[None, :, None]
    gathered = jnp.take(tables.reshape(slots_here * bucket_count, -1), flat_ids, axis=0)
    live = (jnp.arange(ids.shape[2], dtype=jnp.int32)[None, None, :] < lengths[:, :, None]).astype(
        jnp.bfloat16
    )
    return jnp.einsum("gfj,gfje->gfe", live, gathered, preferred_element_type=jnp.float32).astype(
        jnp.bfloat16
    )


def body(
    tables,
    bag_ids,
    bag_lengths,
    slot_field,
    proj_y,
    proj_p,
    linear_w,
    fm_gain,
    w_up,
    w_down,
    out_gain,
    cotangent,
):
    pooled = pool_bags(tables, bag_ids[0], bag_lengths[0])[None]
    received = lax.all_to_all(pooled, "emb", split_axis=1, concat_axis=2, tiled=True)
    slot_embeds = received[0]
    embeds = jnp.zeros_like(slot_embeds).at[:, slot_field].set(slot_embeds)
    samples = embeds.shape[0]
    crossed = jnp.einsum("bfe,fk->bek", embeds, proj_y, preferred_element_type=jnp.float32).astype(
        jnp.bfloat16
    )
    mixing = jnp.einsum("nf,bfe->bne", proj_p, embeds, preferred_element_type=jnp.float32).astype(
        jnp.bfloat16
    )
    inter = jnp.einsum("bne,bek->bnk", mixing, crossed, preferred_element_type=jnp.float32)
    inter_unit, inter_scale = layer_norm(inter)
    inter_norm = (inter_unit * fm_gain).astype(jnp.bfloat16)
    inter_rows = inter_norm.reshape(samples * NF, -1)
    row_total = inter_rows.shape[0]
    up_all, down_all = (
        lax.all_gather(w_up, "wide", axis=0, tiled=True),
        lax.all_gather(w_down, "wide", axis=0, tiled=True),
    )
    gate_pre = jnp.einsum("rk,hk->rh", inter_rows, up_all, preferred_element_type=jnp.float32)
    hidden = jax.nn.silu(gate_pre).astype(jnp.bfloat16)
    ff_rows = jnp.dot(hidden, down_all, preferred_element_type=jnp.float32)
    linear_out = jnp.einsum("lf,bfe->ble", linear_w, embeds, preferred_element_type=jnp.float32)
    summed = jnp.concatenate(
        [ff_rows.reshape(samples, NF, -1), linear_out], axis=1
    ) + embeds.astype(jnp.float32)
    summed_unit, summed_scale = layer_norm(summed)
    layer_out = (summed_unit * out_gain).astype(jnp.bfloat16)
    grad_summed = norm_back(summed_unit, summed_scale, out_gain, cotangent[0].astype(jnp.float32))
    grad_ff = grad_summed[:, :NF].astype(jnp.bfloat16)
    grad_lin = grad_summed[:, NF:].astype(jnp.bfloat16)
    grad_ff_rows = grad_ff.reshape(row_total, -1)
    grad_hidden = jnp.einsum(
        "re,he->rh", grad_ff_rows, down_all, preferred_element_type=jnp.float32
    )
    grad_gate = (grad_hidden * silu_back(gate_pre)).astype(jnp.bfloat16)
    grad_rows = jnp.dot(grad_gate, up_all, preferred_element_type=jnp.float32)
    rank_width = w_up.shape[1]
    up_term = jnp.einsum("rh,rk->hk", grad_gate, inter_rows, preferred_element_type=jnp.float32)
    down_term_part = jnp.einsum(
        "rh,re->he", hidden, grad_ff_rows, preferred_element_type=jnp.float32
    )
    both_terms = lax.psum_scatter(
        jnp.concatenate([up_term, down_term_part], axis=1), "wide", scatter_dimension=0, tiled=True
    )
    up_local = both_terms[:, :rank_width]
    down_local = both_terms[:, rank_width:]
    grad_up, grad_down = lax.psum((up_local, down_local), "emb")
    grad_norm = grad_rows.reshape(samples, NF, -1)
    grad_inter = norm_back(inter_unit, inter_scale, fm_gain, grad_norm).astype(jnp.bfloat16)
    grad_mixing = jnp.einsum(
        "bnk,bek->bne", grad_inter, crossed, preferred_element_type=jnp.float32
    ).astype(jnp.bfloat16)
    grad_crossed = jnp.einsum(
        "bne,bnk->bek", mixing, grad_inter, preferred_element_type=jnp.float32
    ).astype(jnp.bfloat16)
    grad_embeds = grad_summed + jnp.einsum(
        "lf,ble->bfe", linear_w, grad_lin, preferred_element_type=jnp.float32
    )
    grad_embeds = grad_embeds + jnp.einsum(
        "nf,bne->bfe", proj_p, grad_mixing, preferred_element_type=jnp.float32
    )
    grad_embeds = grad_embeds + jnp.einsum(
        "fk,bek->bfe", proj_y, grad_crossed, preferred_element_type=jnp.float32
    )
    grad_embeds = grad_embeds.astype(jnp.bfloat16)
    slot_grads = grad_embeds[:, slot_field]
    returned = lax.all_to_all(slot_grads[None], "emb", split_axis=2, concat_axis=1, tiled=True)
    return (layer_out[None], returned, grad_up, grad_down)


def solution(mesh):
    placed = (
        P("emb", None, None),
        P("wide", None, "emb", None),
        P("wide", None, "emb"),
        P(),
        P(),
        P(),
        P(),
        P(),
        P("wide", None),
        P("wide", None),
        P(),
        P("wide", "emb", None, None),
    )
    return jax.shard_map(
        body,
        mesh=mesh,
        in_specs=placed,
        out_specs=(
            P("wide", "emb", None, None),
            P("wide", None, "emb", None),
            P("wide", None),
            P("wide", None),
        ),
        check_vma=False,
    )
```

profile of v0, /device:TPU:1, one launch (start us, length us, event | category | flops | bytes accessed | tf_op | source)
XLA Modules:
  0.0 923.4 jit_solution(3896068090639616225)
XLA Ops:
  11.6 33.8 %gather_fusion = bf16[8192,256]{1,0:T(8,128)(2,1)} fusion(bf16[8192,256]{1,0:T(8,128)(2,1)} %bitcast.109, s32[8192]{0:T(1024)S(1)} %broadcast_clamp_fusion), kind=kCustom, calls=%fused_computation | custom fusion | bytes 8421376 | tf_op jit(solution)/shard_map/jit(_take)/gather | solution.py:35
  45.4 7.0 reshape.111
  53.4 8.1 fusion
  62.7 12.8 %all-to-all-start = ((bf16[1,128,16,256]{3,2,0,1:T(8,128)(2,1)}), bf16[1,128,16,256]{3,2,0,1:T(8,128)(2,1)S(1)}, u32[]{:S(2)}, u32[]{:S(2)}) async-start(bf16[1,128,16,256]{3,2,0,1:T(8,128)(2,1)} %bitcast.108), calls=%async_computation | async-start | bytes 2097152 | tf_op jit(solution)/shard_map/all_to_all | solution.py:59
  76.9 38.6 %all-to-all-done = bf16[1,128,16,256]{3,2,0,1:T(8,128)(2,1)S(1)} async-done(((bf16[1,128,16,256]{3,2,0,1:T(8,128)(2,1)}), bf16[1,128,16,256]{3,2,0,1:T(8,128)(2,1)S(1)}, u32[]{:S(2)}, u32[]{:S(2)}) %all-to-all-start) | async-done | bytes 1048608 | tf_op jit(solution)/shard_map/all_to_all | solution.py:59
  116.7 13.6 %scatter_fusion = bf16[4,512,256]{2,0,1:T(4,128)(2,1)S(1)} fusion(bf16[4,512,256]{2,0,1:T(4,128)(2,1)S(1)} %broadcast_in_dim.20, s32[512]{0:T(512)S(1)} %compare_select_fusion.2, bf16[512,4,256]{2,1,0:T(4,128)(2,1)S(1)} %copy.69), kind=kCustom, calls=%fused_computation.2 | custom fusion | bytes 3147776 | tf_op jit(solution)/shard_map/scatter | solution.py:61
  137.9 13.1 %multiply_convert_fusion.1 = (bf16[512,8192]{1,0:T(8,128)(2,1)}, f32[512,8192]{1,0:T(8,128)}) fusion(bf16[512,256]{1,0:T(8,128)(2,1)S(1)} %bitcast.114, bf16[8192,256]{1,0:T(8,128)(2,1)} %all-gather.3.cloned.1.call-done), kind=kOutput, calls=%fused_computation.5 | convolution fusion | flops 2168455168 | bytes 29622272 | tf_op jit(solution)/shard_map/rk,hk->rh/dot_general | solution.py:78
  151.0 73.2 %all-gather.5.cloned.1.call-done = bf16[8192,256]{1,0:T(8,128)(2,1)} async-done(((bf16[1024,256]{1,0:T(8,128)(2,1)}), bf16[8192,256]{1,0:T(8,128)(2,1)}) %all-gather.5.cloned.1.call-update) | async-done | bytes 4194320 | tf_op jit(solution)/shard_map/all_gather | solution.py:76
  224.3 6.9 fusion.29
  238.1 5.8 fusion.31
  244.0 13.6 %multiply_convert_fusion = bf16[512,8192]{1,0:T(8,128)(2,1)} fusion(f32[512,8192]{1,0:T(8,128)} %get-tuple-element.33, bf16[512,256]{1,0:T(8,128)(2,1)S(1)} %bitcast.117, bf16[8192,256]{1,0:T(8,128)(2,1)} %all-gather.5.cloned.1.call-done), kind=kOutput, calls=%fused_computation.4 | convolution fusion | flops 2185232384 | bytes 29622272 | tf_op jit(solution)/shard_map/re,he->rh/dot_general | solution.py:91
  257.6 6.0 fusion.30
  263.6 6.2 pad_maximum_fusion
  271.0 7.1 multiply_reduce_fusion.2
  281.5 3.4 fusion.16
  284.9 314.3 %reduce-scatter.2.cloned.1.call-done = f32[1024,512]{0,1:T(8,128)} async-done(((f32[8192,512]{0,1:T(8,128)}), f32[1024,512]{0,1:T(8,128)}) %reduce-scatter.2.cloned.1.call-update) | async-done | bytes 2097168 | tf_op jit(solution)/shard_map/reduce_scatter | solution.py:101
  599.2 3.1 fusion.27
  602.4 4.5 fusion.10
  608.6 3.1 gather_fusion.1
  611.7 9.3 %all-to-all-start.1 = ((bf16[1,4,512,256]{3,1,0,2:T(4,128)(2,1)}), bf16[1,4,512,256]{3,1,0,2:T(4,128)(2,1)S(1)}, u32[]{:S(2)}, u32[]{:S(2)}) async-start(bf16[1,4,512,256]{3,1,0,2:T(4,128)(2,1)} %bitcast.27), calls=%async_computation.1 | async-start | bytes 2097152 | tf_op jit(solution)/shard_map/all_to_all | solution.py:126
  622.4 22.7 %all-to-all-done.1 = bf16[1,4,512,256]{3,1,0,2:T(4,128)(2,1)S(1)} async-done(((bf16[1,4,512,256]{3,1,0,2:T(4,128)(2,1)}), bf16[1,4,512,256]{3,1,0,2:T(4,128)(2,1)S(1)}, u32[]{:S(2)}, u32[]{:S(2)}) %all-to-all-start.1) | async-done | bytes 1048608 | tf_op jit(solution)/shard_map/all_to_all | solution.py:126
  646.3 265.5 %all-reduce.3.cloned.1.call-done = (f32[1024,256]{0,1:T(8,128)}, f32[1024,256]{0,1:T(8,128)}) async-done(((f32[1024,256]{0,1:T(8,128)}, f32[1024,256]{0,1:T(8,128)}), (f32[1024,256]{0,1:T(8,128)}, f32[1024,256]{0,1:T(8,128)})) %all-reduce.3.cloned.1.call-update) | async-done | bytes 2097168 | tf_op jit(solution)/shard_map/psum | solution.py:106
  911.8 2.5 copy.84
  914.3 2.5 copy.85
  (109 shorter events, 32.6 us)
Async XLA Ops:
  7.2 128.8 %copy-start = (bf16[384,512]{1,0:T(8,128)(2,1)S(1)}, bf16[384,512]{1,0:T(8,128)(2,1)}, u32[]{:S(2)}) copy-start(bf16[384,512]{1,0:T(8,128)(2,1)} %param.18) | copy-start | bytes 1179652
  7.2 130.7 %all-gather.3.cloned.1.call-start = ((), (), s32[]{:S(2)}) async-start(), calls=%async_computation.3 | async-start | bytes 4718592 | tf_op jit(solution)/shard_map/all_gather | solution.py:75
  7.9 216.3 %all-gather.5.cloned.1.call-start = ((), (), s32[]{:S(2)}) async-start(), calls=%async_computation.4 | async-start | bytes 4718592 | tf_op jit(solution)/shard_map/all_gather | solution.py:76
  45.4 7.6 copy-start.26
  61.5 14.1 %copy-start.13 = (bf16[1,4,512,256]{3,2,1,0:T(8,128)(2,1)S(1)}, bf16[1,4,512,256]{3,2,1,0:T(8,128)(2,1)}, u32[]{:S(2)}) copy-start(bf16[1,4,512,256]{3,2,1,0:T(8,128)(2,1)} %param.23) | copy-start | bytes 3145732
  61.5 15.4 %copy-start.27 = (s32[512]{0:T(512)S(1)}, s32[512]{0:T(512)}, u32[]{:S(2)}) copy-start(s32[512]{0:T(512)} %param.15) | copy-start | bytes 6148
  62.7 52.7 %all-to-all-start = ((bf16[1,128,16,256]{3,2,0,1:T(8,128)(2,1)}), bf16[1,128,16,256]{3,2,0,1:T(8,128)(2,1)S(1)}, u32[]{:S(2)}, u32[]{:S(2)}) async-start(bf16[1,128,16,256]{3,2,0,1:T(8,128)(2,1)} %bitcast.108), calls=%async_computation | async-start | bytes 2097152 | tf_op jit(solution)/shard_map/all_to_all | solution.py:59
  75.5 523.7 %reduce-scatter.2.cloned.1.call-start = ((), (), s32[]{:S(2)}) async-start(), calls=%async_computation.5 | async-start | bytes 18874368 | tf_op jit(solution)/shard_map/reduce_scatter | solution.py:101
  76.9 39.8 %copy-start.21 = (s32[512]{0:T(512)}, s32[512]{0:T(512)S(1)}, u32[]{:S(2)}) copy-start(s32[512]{0:T(512)S(1)} %compare_select_fusion.2) | copy-start | bytes 6148
  130.2 5.5 copy-start.23
  132.6 3.4 copy-start.9
  136.0 15.0 %copy-start.11 = (bf16[4,128,256]{2,1,0:T(8,128)(2,1)}, bf16[4,128,256]{2,1,0:T(8,128)(2,1)S(1)}, u32[]{:S(2)}) copy-start(bf16[4,128,256]{2,1,0:T(8,128)(2,1)S(1)} %multiply_convert_fusion.4) | copy-start | bytes 786436
  232.2 2.3 copy-start.1
  232.2 2.3 copy-start.25
  244.0 13.6 %copy-start.12 = (bf16[4,128,256]{2,1,0:T(8,128)(2,1)S(1)}, bf16[4,128,256]{2,1,0:T(8,128)(2,1)}, u32[]{:S(2)}) copy-start(bf16[4,128,256]{2,1,0:T(8,128)(2,1)} %copy-done.11) | copy-start | bytes 786436
  269.7 642.0 %all-reduce.3.cloned.1.call-start = ((), (), s32[]{:S(2)}) async-start(), calls=%async_computation.6 | async-start | bytes 4194304 | tf_op jit(solution)/shard_map/psum | solution.py:106
  271.0 7.1 copy-start.4
  271.0 7.1 copy-start.18
  271.0 7.1 copy-start.20
  271.0 8.5 copy-start.6
  271.0 8.5 copy-start.14
  281.5 320.9 %copy-start.2 = (bf16[1,4,512,256]{2,3,1,0:T(8,128)(2,1)S(1)}, bf16[1,4,512,256]{2,3,1,0:T(8,128)(2,1)}, u32[]{:S(2)}) copy-start(bf16[1,4,512,256]{2,3,1,0:T(8,128)(2,1)} %copy.76) | copy-start | bytes 3145732
  606.9 14.2 %copy-start.7 = (bf16[1,4,512,256]{2,3,1,0:T(8,128)(2,1)S(1)}, bf16[1,4,512,256]{2,3,1,0:T(8,128)(2,1)}, u32[]{:S(2)}) copy-start(bf16[1,4,512,256]{2,3,1,0:T(8,128)(2,1)} %get-tuple-element.27) | copy-start | bytes 3145732
  611.7 33.3 %all-to-all-start.1 = ((bf16[1,4,512,256]{3,1,0,2:T(4,128)(2,1)}), bf16[1,4,512,256]{3,1,0,2:T(4,128)(2,1)S(1)}, u32[]{:S(2)}, u32[]{:S(2)}) async-start(bf16[1,4,512,256]{3,1,0,2:T(4,128)(2,1)} %bitcast.27), calls=%async_computation.1 | async-start | bytes 2097152 | tf_op jit(solution)/shard_map/all_to_all | solution.py:126
  (10 other events, 11.5 us)
Sparse Core Ops, SparseCore 0:
  9.8 119.3 all-gather.2
  131.0 93.2 all-gather.4
  269.9 329.3 reduce-scatter.1
  602.5 309.2 all-reduce.2
where the time goes:
time: 924 us; the launch traced here: 923 us
  waiting for transfers between devices  716 us (77%)
  local copies, waits for them, and re-layouts  81 us (9%)
  matrix products  75.5 us (8%)
  starting transfers between devices  22.2 us (2%)
  other arithmetic  14.7 us (2%)
  between operations  14.2 us (2%)
    reduce_scatter x1, waiting for transfers between devices, body(): lax.psum_scatter(jnp.concatenate([up_term, down_term_part], axis=1), 'wid...  314 us
    psum x1, waiting for transfers between devices, body(): grad_up, grad_down = lax.psum((up_local, down_local), 'emb')  265 us
    all_gather x1, waiting for transfers between devices, body(): lax.all_gather(w_down, 'wide', axis=0, tiled=True)  73.2 us
    gather x2, local copies, waits for them, and re-layouts, pool_bags(): jnp.take(tables.reshape(slots_here * bucket_count, -1), flat_ids, axis=0)  40.8 us
    all_to_all x1, waiting for transfers between devices, body(): lax.all_to_all(pooled, 'emb', split_axis=1, concat_axis=2, tiled=True)  38.6 us
    all_to_all x1, waiting for transfers between devices, body(): lax.all_to_all(slot_grads[None], 'emb', split_axis=2, concat_axis=1, tile...  22.7 us
  transfers between devices with their start and end apart: 6, of which 5 were waited for; matrix products, arithmetic and copies ran while one was open for 12% of the time, Pallas kernels for 0%

commit v1 on v0

--- a/solution.py
+++ b/solution.py
@@ -73,7 +73,9 @@
     row_total = inter_rows.shape[0]
     up_all, down_all = (
         lax.all_gather(w_up, "wide", axis=0, tiled=True),
-        lax.all_gather(w_down, "wide", axis=0, tiled=True),
+        jnp.concatenate(
+            lax.all_to_all(jnp.stack([w_down] * lax.axis_size("wide")), "wide", 0, 0), axis=0
+        ),
     )
     gate_pre = jnp.einsum("rk,hk->rh", inter_rows, up_all, preferred_element_type=jnp.float32)
     hidden = jax.nn.silu(gate_pre).astype(jnp.bfloat16)

time: 924 us -> 872 us (0.944)
  waiting for transfers between devices: 716 us -> 619 us
  blocking collectives: 0 us -> 52.5 us
    all_gather x1 -> x0, waiting for transfers between devices: 73.2 us -> none  [body(): lax.all_gather(w_down, 'wide', axis=0, tiled=True)]
    all_to_all x0 -> x1, blocking collectives: none -> 52.5 us  [body(): lax.all_to_all(pooled, 'emb', split_axis=1, concat_axis=2, tiled=True)]
    all_to_all x1, waiting for transfers between devices: 38.6 us -> 17.3 us  [body(): lax.all_to_all(jnp.stack([w_down] * lax.axis_size('wide')), 'wide', 0, 0)]
  transfers between devices with their start and end apart: 6 -> 5, of which waited for: 5 -> 4; matrix products, arithmetic and copies ran while one was open for 12% -> 13% of each run, Pallas kernels for 0% -> 0%
where the time goes in v1:
time: 872 us; the launch traced here: 871 us
  waiting for transfers between devices  619 us (71%)
  local copies, waits for them, and re-layouts  81.6 us (9%)
  matrix products  75.7 us (9%)
  blocking collectives  52.5 us (6%)
  starting transfers between devices  14.7 us (2%)
  between operations  14.2 us (2%)
  other arithmetic  13 us (1%)
    reduce_scatter x1, waiting for transfers between devices, body(): lax.psum_scatter(jnp.concatenate([up_term, down_term_part], axis=1), 'wid...  313 us
    psum x1, waiting for transfers between devices, body(): grad_up, grad_down = lax.psum((up_local, down_local), 'emb')  265 us
    all_to_all x1, blocking collectives, body(): lax.all_to_all(pooled, 'emb', split_axis=1, concat_axis=2, tiled=True)  52.5 us
    gather x2, local copies, waits for them, and re-layouts, pool_bags(): jnp.take(tables.reshape(slots_here * bucket_count, -1), flat_ids, axis=0)  40.7 us
    all_to_all x1, waiting for transfers between devices, body(): lax.all_to_all(slot_grads[None], 'emb', split_axis=2, concat_axis=1, tile...  22.7 us
  transfers between devices with their start and end apart: 5, of which 4 were waited for; matrix products, arithmetic and copies ran while one was open for 13% of the time, Pallas kernels for 0%

profile of v1, /device:TPU:1, one launch (start us, length us, event | category | flops | bytes accessed | tf_op | source)
XLA Modules:
  0.0 871.0 jit_solution(16606223794085552465)
XLA Ops:
  10.8 33.7 %gather_fusion = bf16[8192,256]{1,0:T(8,128)(2,1)} fusion(bf16[8192,256]{1,0:T(8,128)(2,1)} %bitcast.112, s32[8192]{0:T(1024)S(1)} %broadcast_clamp_fusion), kind=kCustom, calls=%fused_computation | custom fusion | bytes 8421376 | tf_op jit(solution)/shard_map/jit(_take)/gather | solution.py:35
  44.5 7.0 reshape.115
  52.5 8.1 fusion
  60.9 52.5 %all_to_all.38 = bf16[1,128,16,256]{3,2,0,1:T(8,128)(2,1)S(1)} all-to-all(bf16[1,128,16,256]{3,2,0,1:T(8,128)(2,1)S(1)} %bitcast.114), channel_id=1, replica_groups=mesh['emb'=32,'wide'=8] {'emb'}, dimensions={1} | all-to-all | bytes 2097152 | tf_op jit(solution)/shard_map/all_to_all | solution.py:59
  115.8 4.7 all-to-all-start.1
  123.3 13.6 %scatter_fusion = bf16[4,512,256]{2,0,1:T(4,128)(2,1)S(1)} fusion(bf16[4,512,256]{2,0,1:T(4,128)(2,1)S(1)} %broadcast_in_dim.20, s32[512]{0:T(512)S(1)} %compare_select_fusion.2, bf16[512,4,256]{2,1,0:T(4,128)(2,1)S(1)} %copy.69), kind=kCustom, calls=%fused_computation.2 | custom fusion | bytes 3147776 | tf_op jit(solution)/shard_map/scatter | solution.py:61
  144.6 13.1 %multiply_convert_fusion.1 = (bf16[512,8192]{1,0:T(8,128)(2,1)}, f32[512,8192]{1,0:T(8,128)}) fusion(bf16[512,256]{1,0:T(8,128)(2,1)S(1)} %bitcast.119, bf16[8192,256]{1,0:T(8,128)(2,1)} %all-gather.2.cloned.1.call-done), kind=kOutput, calls=%fused_computation.5 | convolution fusion | flops 2168455168 | bytes 29622272 | tf_op jit(solution)/shard_map/rk,hk->rh/dot_general | solution.py:80
  157.7 17.3 %all-to-all-done.1 = bf16[8,1024,256]{2,1,0:T(8,128)(2,1)} async-done(((bf16[8,1024,256]{2,1,0:T(8,128)(2,1)}), bf16[8,1024,256]{2,1,0:T(8,128)(2,1)}, u32[]{:S(2)}, u32[]{:S(2)}) %all-to-all-start.1) | async-done | bytes 4194336 | tf_op jit(solution)/shard_map/all_to_all | solution.py:77
  175.0 7.3 fusion.29
  187.2 5.8 fusion.31
  193.1 13.6 %multiply_convert_fusion = bf16[512,8192]{1,0:T(8,128)(2,1)} fusion(f32[512,8192]{1,0:T(8,128)} %get-tuple-element.33, bf16[512,256]{1,0:T(8,128)(2,1)S(1)} %bitcast.122, bf16[8192,256]{1,0:T(8,128)(2,1)} %bitcast.15), kind=kOutput, calls=%fused_computation.4 | convolution fusion | flops 2185232384 | bytes 29622272 | tf_op jit(solution)/shard_map/re,he->rh/dot_general | solution.py:93
  206.6 6.0 fusion.30
  212.6 6.1 pad_maximum_fusion
  220.0 7.1 multiply_reduce_fusion.2
  230.6 3.2 fusion.16
  233.8 313.2 %reduce-scatter.2.cloned.1.call-done = f32[1024,512]{0,1:T(8,128)} async-done(((f32[8192,512]{0,1:T(8,128)}), f32[1024,512]{0,1:T(8,128)}) %reduce-scatter.2.cloned.1.call-update) | async-done | bytes 2097168 | tf_op jit(solution)/shard_map/reduce_scatter | solution.py:103
  547.0 3.1 fusion.27
  550.2 4.5 fusion.10
  556.5 3.1 gather_fusion.1
  559.5 9.3 %all-to-all-start.2 = ((bf16[1,4,512,256]{3,1,0,2:T(4,128)(2,1)}), bf16[1,4,512,256]{3,1,0,2:T(4,128)(2,1)S(1)}, u32[]{:S(2)}, u32[]{:S(2)}) async-start(bf16[1,4,512,256]{3,1,0,2:T(4,128)(2,1)} %bitcast.29), calls=%async_computation.2 | async-start | bytes 2097152 | tf_op jit(solution)/shard_map/all_to_all | solution.py:128
  570.2 22.7 %all-to-all-done.2 = bf16[1,4,512,256]{3,1,0,2:T(4,128)(2,1)S(1)} async-done(((bf16[1,4,512,256]{3,1,0,2:T(4,128)(2,1)}), bf16[1,4,512,256]{3,1,0,2:T(4,128)(2,1)S(1)}, u32[]{:S(2)}, u32[]{:S(2)}) %all-to-all-start.2) | async-done | bytes 1048608 | tf_op jit(solution)/shard_map/all_to_all | solution.py:128
  594.1 265.3 %all-reduce.3.cloned.1.call-done = (f32[1024,256]{0,1:T(8,128)}, f32[1024,256]{0,1:T(8,128)}) async-done(((f32[1024,256]{0,1:T(8,128)}, f32[1024,256]{0,1:T(8,128)}), (f32[1024,256]{0,1:T(8,128)}, f32[1024,256]{0,1:T(8,128)})) %all-reduce.3.cloned.1.call-update) | async-done | bytes 2097168 | tf_op jit(solution)/shard_map/psum | solution.py:108
  859.4 2.5 copy.84
  861.9 2.5 copy.85
  (111 shorter events, 31.4 us)
Async XLA Ops:
  7.2 135.5 %copy-start = (bf16[384,512]{1,0:T(8,128)(2,1)S(1)}, bf16[384,512]{1,0:T(8,128)(2,1)}, u32[]{:S(2)}) copy-start(bf16[384,512]{1,0:T(8,128)(2,1)} %param.18) | copy-start | bytes 1179652
  7.2 137.4 %all-gather.2.cloned.1.call-start = ((), (), s32[]{:S(2)}) async-start(), calls=%async_computation.4 | async-start | bytes 4718592 | tf_op jit(solution)/shard_map/all_gather | solution.py:75
  44.5 7.6 copy-start.28
  60.6 52.8 %copy-start.15 = (bf16[1024,256]{1,0:T(8,128)(2,1)S(1)}, bf16[1024,256]{1,0:T(8,128)(2,1)}, u32[]{:S(2)}) copy-start(bf16[1024,256]{1,0:T(8,128)(2,1)} %param.21) | copy-start | bytes 1572868
  115.8 5.0 copy-start.14
  115.8 6.3 copy-start.29
  115.8 59.2 %all-to-all-start.1 = ((bf16[8,1024,256]{2,1,0:T(8,128)(2,1)}), bf16[8,1024,256]{2,1,0:T(8,128)(2,1)}, u32[]{:S(2)}, u32[]{:S(2)}) async-start(bf16[8,1024,256]{2,1,0:T(8,128)(2,1)} %stack.2), calls=%async_computation.1 | async-start | bytes 8388608 | tf_op jit(solution)/shard_map/all_to_all | solution.py:77
  120.5 426.5 %reduce-scatter.2.cloned.1.call-start = ((), (), s32[]{:S(2)}) async-start(), calls=%async_computation.5 | async-start | bytes 18874368 | tf_op jit(solution)/shard_map/reduce_scatter | solution.py:103
  136.9 5.6 copy-start.25
  139.2 3.5 copy-start.10
  140.7 2.0 copy-start.6
  142.7 15.0 %copy-start.12 = (bf16[4,128,256]{2,1,0:T(8,128)(2,1)}, bf16[4,128,256]{2,1,0:T(8,128)(2,1)S(1)}, u32[]{:S(2)}) copy-start(bf16[4,128,256]{2,1,0:T(8,128)(2,1)S(1)} %multiply_convert_fusion.4) | copy-start | bytes 786436
  175.0 7.3 copy-start.5
  184.2 1.9 copy-start.17
  193.1 13.6 %copy-start.13 = (bf16[4,128,256]{2,1,0:T(8,128)(2,1)S(1)}, bf16[4,128,256]{2,1,0:T(8,128)(2,1)}, u32[]{:S(2)}) copy-start(bf16[4,128,256]{2,1,0:T(8,128)(2,1)} %copy-done.12) | copy-start | bytes 786436
  218.8 640.6 %all-reduce.3.cloned.1.call-start = ((), (), s32[]{:S(2)}) async-start(), calls=%async_computation.6 | async-start | bytes 4194304 | tf_op jit(solution)/shard_map/psum | solution.py:108
  220.0 7.1 copy-start.4
  220.0 7.1 copy-start.20
  220.0 7.1 copy-start.22
  220.0 8.5 copy-start.7
  220.0 8.5 copy-start.16
  230.5 319.6 %copy-start.2 = (bf16[1,4,512,256]{2,3,1,0:T(8,128)(2,1)S(1)}, bf16[1,4,512,256]{2,3,1,0:T(8,128)(2,1)}, u32[]{:S(2)}) copy-start(bf16[1,4,512,256]{2,3,1,0:T(8,128)(2,1)} %copy.76) | copy-start | bytes 3145732
  554.7 14.2 %copy-start.8 = (bf16[1,4,512,256]{2,3,1,0:T(8,128)(2,1)S(1)}, bf16[1,4,512,256]{2,3,1,0:T(8,128)(2,1)}, u32[]{:S(2)}) copy-start(bf16[1,4,512,256]{2,3,1,0:T(8,128)(2,1)} %get-tuple-element.27) | copy-start | bytes 3145732
  559.5 33.4 %all-to-all-start.2 = ((bf16[1,4,512,256]{3,1,0,2:T(4,128)(2,1)}), bf16[1,4,512,256]{3,1,0,2:T(4,128)(2,1)S(1)}, u32[]{:S(2)}, u32[]{:S(2)}) async-start(bf16[1,4,512,256]{3,1,0,2:T(4,128)(2,1)} %bitcast.29), calls=%async_computation.2 | async-start | bytes 2097152 | tf_op jit(solution)/shard_map/all_to_all | solution.py:128
  (11 other events, 11.3 us)
Sparse Core Ops, SparseCore 0:
  9.8 122.8 all-gather.1
  218.9 328.0 reduce-scatter.1
  550.3 309.0 all-reduce.2
